TPU v7x, 32 devices: a whole 2x2x4 slice. The times are simulated.
32 devices in a mesh: vocab: 8 (over y, x, core), width: 4 (over z).
Axes of the slice: x: 2, y: 2, z: 4, core: 2. Of those that a mesh axis runs over, the one named last changes fastest.
Arguments:
- hidden: bfloat16 [256, 2880], P('width'), may hold values from -60 to 60
- gain: float32 [2880], replicated, may hold values from 0.1 to 1.9
- unembed: bfloat16 [2880, 50176], P('width', 'vocab'), may hold values from -8 to 8
- targets: int32 [256], replicated, may hold values from 0 to 50175
- seq_ids: int32 [256], replicated, may hold values from 0 to 47, as said below
Outputs:
- log_normalizer: float32 [256], P('width')
- entropy: float32 [256], P('width')
- token_logprob: float32 [256], P('width')
- seq_mean: float32 [48], replicated
Inputs may be any that keep to these rules, and one draw needn't show every extreme that they name: `seq_ids`: rows of one sequence are consecutive and ids never fall; every sequence has at least one row.
All inputs are finite; a program needn't handle non-finite values.
Results may differ from a plain program's by a relative error of at most 0.0014.
Values may be sent and summed in bfloat16 or wider, within the bound.
A program may use at most 128 MiB of HBM per device.

v0:
```python
import functools

import jax
import jax.numpy as jnp
from jax import lax
from jax.experimental import pallas as pl
from jax.experimental.pallas import tpu as pltpu
from jax.sharding import PartitionSpec as P

SEQS = 48
LANES = 128
LAG = 5
GROUPS = 2
LOWEST = -1e38
MESH = pl.DeviceIdType.MESH


def kernel(
    n, nv, hidden_ref, gain_ref, unembed_ref, targets_ref, seq_ref, out_ref,
    weights, blocks, rows_in, buf, target_cols, state, packed, gathered, final,
    w_sem, own_sem, x_send, x_recv, p_send, p_recv, c_send, c_recv, v_send, v_recv, f_send, f_recv,
):
    me = lax.axis_index("width")
    my_vocab = lax.axis_index("vocab")
    own_rows, width_dim = hidden_ref.shape
    share = width_dim // n
    half = (n // 2) * own_rows
    chunks = unembed_ref.shape[1] // LANES
    last = n - 1
    group_blocks = n // 2 // GROUPS
    group_rows = group_blocks * own_rows
    items = GROUPS * chunks
    slots = last * LAG + 1

    early = chunks // 7 * LANES
    loads = []
    for k, cols in enumerate((pl.ds(0, early), pl.ds(early, chunks * LANES - early))):
        loads.append(
            pltpu.make_async_copy(unembed_ref.at[:, cols], weights.at[:, cols], w_sem.at[k])
        )
        loads[k].start()

    barrier = pltpu.get_barrier_semaphore()
    for k in range(1, n):
        pl.semaphore_signal(
            barrier, inc=1, device_id={"width": lax.rem(me + k, n)}, device_id_type=MESH
        )
    for k in range(1, nv):
        pl.semaphore_signal(
            barrier, inc=1, device_id={"vocab": lax.rem(my_vocab + k, nv)}, device_id_type=MESH
        )

    values = hidden_ref[...].astype(jnp.float32)
    square = jnp.mean(values * values, axis=1, keepdims=True)
    normed = (values * lax.rsqrt(square + 1e-05) * gain_ref[...][None, :]).astype(jnp.bfloat16)
    for j in range(n):
        blocks[j] = normed[:, j * share : (j + 1) * share]

    pl.semaphore_wait(barrier, n - 1 + nv - 1)

    my_part = pl.ds(pl.multiple_of(lax.rem(my_vocab, 2) * (own_rows // 2), own_rows // 2), own_rows // 2)
    other_part = pl.ds(
        pl.multiple_of((1 - lax.rem(my_vocab, 2)) * (own_rows // 2), own_rows // 2), own_rows // 2
    )
    partner = my_vocab + 1 - 2 * lax.rem(my_vocab, 2)

    def row_copy(peer, source):
        return pltpu.make_async_remote_copy(
            src_ref=blocks.at[peer, my_part],
            dst_ref=rows_in.at[source, my_part],
            send_sem=x_send.at[peer],
            recv_sem=x_recv.at[source],
            device_id={"width": peer},
            device_id_type=MESH,
        )

    def pass_rows(source, part):
        return pltpu.make_async_remote_copy(
            src_ref=rows_in.at[source, part],
            dst_ref=rows_in.at[source, part],
            send_sem=p_send.at[source],
            recv_sem=p_recv.at[source],
            device_id={"vocab": partner},
            device_id_type=MESH,
        )

    def send_rows():
        for k in range(1, n):
            row_copy(lax.rem(me + jnp.where(me < n // 2, k, n - k), n), me).start()

    rows_now = jnp.where(me < n // 2, me, last - me) < group_blocks

    @pl.when(rows_now)
    def _():
        send_rows()

    own = pltpu.make_async_copy(blocks.at[me], rows_in.at[me], own_sem)
    own.start()

    target_row = targets_ref[...].astype(jnp.float32)
    target_all = jnp.transpose(jnp.broadcast_to(target_row, (LANES, 2 * half)))
    target_cols[0] = target_all[:half]
    target_cols[1] = target_all[half:]
    state[0] = jnp.full((half, LANES), LOWEST, jnp.float32)
    for k in range(1, 4):
        state[k] = jnp.zeros((half, LANES), jnp.float32)

    own.wait()
    loads[0].wait()

    def chunk_copy(side, c, peer):
        return pltpu.make_async_remote_copy(
            src_ref=buf.at[side, c],
            dst_ref=buf.at[side, c],
            send_sem=c_send.at[side, lax.rem(c, slots)],
            recv_sem=c_recv.at[side, lax.rem(c, slots)],
            device_id={"width": peer},
            device_id_type=MESH,
        )

    first_col = my_vocab * (chunks * LANES)
    lane = lax.broadcasted_iota(jnp.int32, (half, LANES), 1)
    item_lane = lax.broadcasted_iota(jnp.int32, (group_rows, LANES), 1)

    def partial_logits(first_block, c):
        cols = pl.ds(pl.multiple_of(c * LANES, LANES), LANES)
        x = rows_in[pl.ds(first_block, group_blocks)].reshape(group_rows, share)
        return jnp.dot(x, weights[:, cols], preferred_element_type=jnp.float32)

    def take_stats(side, first_block, c, logits):
        rows = pl.ds(pl.multiple_of((first_block - side * (n // 2)) * own_rows, 8), group_rows)
        column = (first_col + c * LANES + item_lane).astype(jnp.float32)
        old_max = state[0, rows]
        new_max = jnp.maximum(old_max, logits)
        scale = jnp.exp(old_max - new_max)
        shifted = jnp.exp(logits - new_max)
        state[0, rows] = new_max
        state[1, rows] = state[1, rows] * scale + shifted
        state[2, rows] = state[2, rows] * scale + shifted * logits
        state[3, rows] = state[3, rows] + jnp.where(column == target_cols[side, rows], logits, 0.0)

    def advance(side, item, head, tail, peer):
        @pl.when((item >= 0) & (item < items))
        def _():
            group = item // chunks
            c = item - group * chunks
            first_block = group * group_blocks if side == 0 else n - (group + 1) * group_blocks
            for g in range(GROUPS):
                start = g * group_blocks if side == 0 else n - (g + 1) * group_blocks

                @pl.when(item == g * (chunks // 2))
                def _():
                    for w in range(start, start + group_blocks):

                        @pl.when(me != w)
                        def _():
                            row_copy(w, w).wait_recv()
                            pass_rows(w, my_part).start()

                @pl.when(item == g * chunks)
                def _():
                    for w in range(start, start + group_blocks):

                        @pl.when(me != w)
                        def _():
                            pass_rows(w, other_part).wait_recv()

            mine = partial_logits(first_block, c)

            @pl.when((me != tail) & (item >= slots))
            def _():
                chunk_copy(side, item - slots, peer).wait_send()

            @pl.when(me == head)
            def _():
                buf[side, item] = mine
                chunk_copy(side, item, peer).start()

            @pl.when(me != head)
            def _():
                chunk_copy(side, item, peer).wait_recv()
                total = buf[side, item] + mine

                @pl.when(me != tail)
                def _():
                    buf[side, item] = total
                    chunk_copy(side, item, peer).start()

                @pl.when(me == tail)
                def _():
                    take_stats(side, first_block, c, total)

    down = lax.rem(me + n - 1, n)
    up = lax.rem(me + 1, n)

    def step(s, carry):
        @pl.when(s == 1)
        def _():
            loads[1].wait()

        @pl.when((s == 2 * LAG) & jnp.logical_not(rows_now))
        def _():
            send_rows()

        advance(0, s - me * LAG, 0, last, up)
        advance(1, s - (last - me) * LAG, last, 0, down)
        return carry

    lax.fori_loop(0, items + last * LAG, step, 0)

    def stats_copy(peer, source):
        return pltpu.make_async_remote_copy(
            src_ref=packed.at[0],
            dst_ref=gathered.at[source],
            send_sem=v_send.at[peer],
            recv_sem=v_recv.at[source],
            device_id={"vocab": peer},
            device_id_type=MESH,
        )

    def final_copy(side, peer):
        return pltpu.make_async_remote_copy(
            src_ref=packed.at[1],
            dst_ref=final.at[side],
            send_sem=f_send.at[peer],
            recv_sem=f_recv.at[side],
            device_id={"width": peer},
            device_id_type=MESH,
        )

    def finish(side):
        lane_max = state[0]
        row_max = jnp.max(lane_max, axis=1, keepdims=True)
        scale = jnp.exp(lane_max - row_max)
        columns = (
            row_max,
            jnp.sum(state[1] * scale, axis=1, keepdims=True),
            jnp.sum(state[2] * scale, axis=1, keepdims=True),
            jnp.sum(state[3], axis=1, keepdims=True),
        )
        wide = jnp.zeros((half, LANES), jnp.float32)
        for k in range(4):
            wide = jnp.where(lane == k, columns[k], wide)
        flat = jnp.transpose(wide)[:8]
        packed[0] = flat
        for k in range(1, nv):
            stats_copy(lax.rem(my_vocab + k, nv), my_vocab).start()
        gathered[my_vocab] = flat
        for k in range(1, nv):
            peer = lax.rem(my_vocab + k, nv)
            stats_copy(peer, peer).wait_recv()
        parts = [gathered[v] for v in range(nv)]
        top = functools.reduce(jnp.maximum, [part[0:1] for part in parts])
        total = jnp.zeros_like(top)
        weighted = jnp.zeros_like(top)
        target = jnp.zeros_like(top)
        for part in parts:
            factor = jnp.exp(part[0:1] - top)
            total = total + part[1:2] * factor
            weighted = weighted + part[2:3] * factor
            target = target + part[3:4]
        log_normalizer = top + jnp.log(total)
        rows = lax.broadcasted_iota(jnp.int32, (8, half), 0)
        result = jnp.where(
            rows == 0,
            log_normalizer,
            jnp.where(rows == 1, log_normalizer - weighted / total, target - log_normalizer),
        )
        packed[1] = result
        for k in range(1, n):
            final_copy(side, lax.rem(me + k, n)).start()
        final[side] = result

    @pl.when(me == last)
    def _():
        finish(0)

    @pl.when(me == 0)
    def _():
        finish(1)

    @pl.when(me != last)
    def _():
        final_copy(0, 0).wait_recv()

    @pl.when(me != 0)
    def _():
        final_copy(1, 0).wait_recv()

    ids = lax.broadcasted_iota(jnp.int32, (LANES, half), 0)
    sums = jnp.zeros((LANES, 1), jnp.float32)
    counts = jnp.zeros((LANES, 1), jnp.float32)
    for side in range(2):
        member = ids == seq_ref[:, side * half : (side + 1) * half]
        sums = sums + jnp.sum(jnp.where(member, final[side, 2:3], 0.0), axis=1, keepdims=True)
        counts = counts + jnp.sum(member.astype(jnp.float32), axis=1, keepdims=True)
    means = sums / jnp.maximum(counts, 1.0)
    out_ref[...] = jnp.zeros_like(out_ref)
    out_ref[3:4, :] = jnp.transpose(jnp.broadcast_to(means, (LANES, LANES)))[0:1]
    for w in range(n):

        @pl.when(me == w)
        def _():
            start = (w % (n // 2)) * own_rows
            out_ref[0:3, 0:own_rows] = final[w // (n // 2), 0:3, start : start + own_rows]

    for k in range(1, n):
        row_copy(lax.rem(me + k, n), me).wait_send()
        pass_rows(lax.rem(me + k, n), my_part).wait_send()

    def drain(c, carry):
        @pl.when(me != last)
        def _():
            chunk_copy(0, c, up).wait_send()

        @pl.when(me != 0)
        def _():
            chunk_copy(1, c, down).wait_send()

        return carry

    lax.fori_loop(max(items - slots, 0), items, drain, 0)

    @pl.when((me == 0) | (me == last))
    def _():
        for k in range(1, nv):
            stats_copy(lax.rem(my_vocab + k, nv), my_vocab).wait_send()
        for k in range(1, n):
            final_copy(0, lax.rem(me + k, n)).wait_send()


def solution(mesh):
    n, nv = mesh.shape["width"], mesh.shape["vocab"]

    def local(hidden, gain, unembed, targets, seq_ids):
        own_rows, width_dim = hidden.shape
        share, columns = unembed.shape
        half = (n // 2) * own_rows
        items = GROUPS * (columns // LANES)
        vmem = pl.BlockSpec(memory_space=pltpu.VMEM)
        out = pl.pallas_call(
            functools.partial(kernel, n, nv),
            out_shape=jax.ShapeDtypeStruct((8, LANES), jnp.float32),
            in_specs=[vmem, vmem, pl.BlockSpec(memory_space=pl.ANY), vmem, vmem],
            out_specs=vmem,
            scratch_shapes=[
                pltpu.VMEM((share, columns), jnp.bfloat16),
                pltpu.VMEM((n, own_rows, share), jnp.bfloat16),
                pltpu.VMEM((n, own_rows, share), jnp.bfloat16),
                pltpu.VMEM((2, items, half // GROUPS, LANES), jnp.float32),
                pltpu.VMEM((2, half, LANES), jnp.float32),
                pltpu.VMEM((4, half, LANES), jnp.float32),
                pltpu.VMEM((2, 8, half), jnp.float32),
                pltpu.VMEM((nv, 8, half), jnp.float32),
                pltpu.VMEM((2, 8, half), jnp.float32),
                pltpu.SemaphoreType.DMA((2,)),
                pltpu.SemaphoreType.DMA,
                pltpu.SemaphoreType.DMA((n,)),
                pltpu.SemaphoreType.DMA((n,)),
                pltpu.SemaphoreType.DMA((n,)),
                pltpu.SemaphoreType.DMA((n,)),
                pltpu.SemaphoreType.DMA((2, (n - 1) * LAG + 1)),
                pltpu.SemaphoreType.DMA((2, (n - 1) * LAG + 1)),
                pltpu.SemaphoreType.DMA((nv,)),
                pltpu.SemaphoreType.DMA((nv,)),
                pltpu.SemaphoreType.DMA((n,)),
                pltpu.SemaphoreType.DMA((2,)),
            ],
            compiler_params=pltpu.CompilerParams(
                collective_id=0, has_side_effects=True, vmem_limit_bytes=66_000_000
            ),
        )(hidden, gain, unembed, targets[None, :], seq_ids[None, :])
        return out[0, :own_rows], out[1, :own_rows], out[2, :own_rows], out[3, :SEQS]

    return jax.shard_map(
        local,
        mesh=mesh,
        in_specs=(P("width", None), P(), P("width", "vocab"), P(), P()),
        out_specs=(P("width"), P("width"), P("width"), P()),
        check_vma=False,
    )
```

profile of v0, /device:TPU:0, one launch (start us, length us, event | category | flops | bytes accessed | tf_op | source)
XLA Modules:
  0.0 100.3 jit_solution(10837190758252981300)
XLA Ops:
  0.6 97.2 %shard_map.84 = f32[8,128]{1,0:T(8,128)} custom-call(bf16[64,2880]{1,0:T(8,128)(2,1)} %hidden_ref.1, f32[2880]{0:T(1024)} %gain_ref.1, bf16[720,6272]{1,0:T(8,128)(2,1)} %unembed_ref.1, s32[1,256]{1,0:T(1,128)} %bitcast.10, s32[1,256]{1,0:T(1,128)} %bitcast.11), custom_call_target="tpu_custom_call" | custom-call | tf_op jit(solution)/shard_map/pallas_call | solution.py:341
  97.9 1.3 %slice_bitcast_fusion.1 = (f32[64]{0:T(128)}, f32[64]{0:T(128)}, f32[64]{0:T(128)}) fusion(f32[8,128]{1,0:T(8,128)} %shard_map.84), kind=kLoop, calls=%fused_computation.1 | loop fusion | bytes 1536 | tf_op jit(solution)/shard_map/squeeze | solution.py:373
  99.2 1.2 %slice_bitcast_fusion = f32[48]{0:T(128)} fusion(f32[8,128]{1,0:T(8,128)} %shard_map.84), kind=kLoop, calls=%fused_computation | loop fusion | bytes 384 | tf_op jit(solution)/shard_map/squeeze | solution.py:373
where the time goes:
time: 101 us; the launch traced here: 100 us
  Pallas kernels  97.2 us (96%)
  local copies, waits for them, and re-layouts  2.49 us (2%)
    pallas_call x1, Pallas kernels, local(): pl.pallas_call(functools.partial(kernel, n, nv), out_shape=jax.ShapeDtype...  97.2 us

commit v1 on v0

--- a/solution.py
+++ b/solution.py
@@ -9,16 +9,19 @@
 
 SEQS = 48
 LANES = 128
-LAG = 5
+LAG = 7
 GROUPS = 2
 LOWEST = -1e38
+LEVELS = 32760.0
+TINY = 1e-30
 MESH = pl.DeviceIdType.MESH
 
 
 def kernel(
     n, nv, hidden_ref, gain_ref, unembed_ref, targets_ref, seq_ref, out_ref,
-    weights, blocks, rows_in, buf, target_cols, state, packed, gathered, final,
-    w_sem, own_sem, x_send, x_recv, p_send, p_recv, c_send, c_recv, v_send, v_recv, f_send, f_recv,
+    weights, blocks, rows_in, buf, part, bound, steps, target_cols, state, packed, gathered, final,
+    w_sem, own_sem, x_send, x_recv, p_send, p_recv, c_send, c_recv, b_send, b_recv,
+    v_send, v_recv, f_send, f_recv,
 ):
     me = lax.axis_index("width")
     my_vocab = lax.axis_index("vocab")
@@ -31,8 +34,9 @@
     group_rows = group_blocks * own_rows
     items = GROUPS * chunks
     slots = last * LAG + 1
-
-    early = chunks // 7 * LANES
+    tile = tile_of(chunks)
+
+    early = tile * LANES
     loads = []
     for k, cols in enumerate((pl.ds(0, early), pl.ds(early, chunks * LANES - early))):
         loads.append(
@@ -122,10 +126,55 @@
     lane = lax.broadcasted_iota(jnp.int32, (half, LANES), 1)
     item_lane = lax.broadcasted_iota(jnp.int32, (group_rows, LANES), 1)
 
-    def partial_logits(first_block, c):
-        cols = pl.ds(pl.multiple_of(c * LANES, LANES), LANES)
+    def bound_copy(side, t, peer):
+        return pltpu.make_async_remote_copy(
+            src_ref=bound.at[side, t],
+            dst_ref=bound.at[side, t],
+            send_sem=b_send.at[side, t],
+            recv_sem=b_recv.at[side, t],
+            device_id={"width": peer},
+            device_id_type=MESH,
+        )
+
+    def by_vreg(values):
+        return values.reshape(group_rows // 8, 8, LANES)
+
+    def partial_tile(side, first_block, c, t, head, tail, peer):
+        cols = pl.ds(pl.multiple_of(c * LANES, LANES), tile * LANES)
         x = rows_in[pl.ds(first_block, group_blocks)].reshape(group_rows, share)
-        return jnp.dot(x, weights[:, cols], preferred_element_type=jnp.float32)
+        logits = jnp.dot(x, weights[:, cols], preferred_element_type=jnp.float32)
+        peak = jnp.full((8, LANES), TINY, jnp.float32)
+        for j in range(tile):
+            piece = logits[:, j * LANES : (j + 1) * LANES]
+            part[side, j] = piece
+            peak = jnp.maximum(peak, jnp.max(jnp.abs(by_vreg(piece)), axis=0))
+
+        def announce(limit):
+            bound[side, t] = limit
+            steps[side, 1] = LEVELS / limit
+            bound_copy(side, t, peer).start()
+
+        @pl.when(me == head)
+        def _():
+            announce(peak)
+
+        @pl.when(me != head)
+        def _():
+            bound_copy(side, t, peer).wait_recv()
+            incoming = bound[side, t]
+            steps[side, 0] = incoming * (1.0 / LEVELS)
+
+            @pl.when(me != tail)
+            def _():
+                announce(incoming + peak)
+
+    def to_codes(side, values):
+        scaled = by_vreg(values) * steps[side, 1][None]
+        return jnp.round(scaled).astype(jnp.int32).astype(jnp.int16).reshape(group_rows, LANES)
+
+    def from_codes(side, codes):
+        values = by_vreg(codes.astype(jnp.int32).astype(jnp.float32)) * steps[side, 0][None]
+        return values.reshape(group_rows, LANES)
 
     def take_stats(side, first_block, c, logits):
         rows = pl.ds(pl.multiple_of((first_block - side * (n // 2)) * own_rows, 8), group_rows)
@@ -165,7 +214,11 @@
                         def _():
                             pass_rows(w, other_part).wait_recv()
 
-            mine = partial_logits(first_block, c)
+            k = lax.rem(item, tile)
+
+            @pl.when(k == 0)
+            def _():
+                partial_tile(side, first_block, c, item // tile, head, tail, peer)
 
             @pl.when((me != tail) & (item >= slots))
             def _():
@@ -173,17 +226,17 @@
 
             @pl.when(me == head)
             def _():
-                buf[side, item] = mine
+                buf[side, item] = to_codes(side, part[side, k])
                 chunk_copy(side, item, peer).start()
 
             @pl.when(me != head)
             def _():
                 chunk_copy(side, item, peer).wait_recv()
-                total = buf[side, item] + mine
+                total = from_codes(side, buf[side, item]) + part[side, k]
 
                 @pl.when(me != tail)
                 def _():
-                    buf[side, item] = total
+                    buf[side, item] = to_codes(side, total)
                     chunk_copy(side, item, peer).start()
 
                 @pl.when(me == tail)
@@ -321,12 +374,29 @@
 
     lax.fori_loop(max(items - slots, 0), items, drain, 0)
 
+    def drain_bounds(t, carry):
+        @pl.when(me != last)
+        def _():
+            bound_copy(0, t, up).wait_send()
+
+        @pl.when(me != 0)
+        def _():
+            bound_copy(1, t, down).wait_send()
+
+        return carry
+
+    lax.fori_loop(0, items // tile, drain_bounds, 0)
+
     @pl.when((me == 0) | (me == last))
     def _():
         for k in range(1, nv):
             stats_copy(lax.rem(my_vocab + k, nv), my_vocab).wait_send()
         for k in range(1, n):
             final_copy(0, lax.rem(me + k, n)).wait_send()
+
+
+def tile_of(chunks):
+    return max(k for k in range(1, 9) if chunks % k == 0)
 
 
 def solution(mesh):
@@ -337,6 +407,7 @@
         share, columns = unembed.shape
         half = (n // 2) * own_rows
         items = GROUPS * (columns // LANES)
+        tile = tile_of(columns // LANES)
         vmem = pl.BlockSpec(memory_space=pltpu.VMEM)
         out = pl.pallas_call(
             functools.partial(kernel, n, nv),
@@ -347,7 +418,10 @@
                 pltpu.VMEM((share, columns), jnp.bfloat16),
                 pltpu.VMEM((n, own_rows, share), jnp.bfloat16),
                 pltpu.VMEM((n, own_rows, share), jnp.bfloat16),
-                pltpu.VMEM((2, items, half // GROUPS, LANES), jnp.float32),
+                pltpu.VMEM((2, items, half // GROUPS, LANES), jnp.int16),
+                pltpu.VMEM((2, tile, half // GROUPS, LANES), jnp.float32),
+                pltpu.VMEM((2, items // tile, 8, LANES), jnp.float32),
+                pltpu.VMEM((2, 2, 8, LANES), jnp.float32),
                 pltpu.VMEM((2, half, LANES), jnp.float32),
                 pltpu.VMEM((4, half, LANES), jnp.float32),
                 pltpu.VMEM((2, 8, half), jnp.float32),
@@ -361,6 +435,8 @@
                 pltpu.SemaphoreType.DMA((n,)),
                 pltpu.SemaphoreType.DMA((2, (n - 1) * LAG + 1)),
                 pltpu.SemaphoreType.DMA((2, (n - 1) * LAG + 1)),
+                pltpu.SemaphoreType.DMA((2, items // tile)),
+                pltpu.SemaphoreType.DMA((2, items // tile)),
                 pltpu.SemaphoreType.DMA((nv,)),
                 pltpu.SemaphoreType.DMA((nv,)),
                 pltpu.SemaphoreType.DMA((n,)),

time: 101 us -> 71.8 us (0.71)
  Pallas kernels: 97.2 us -> 68.4 us
    pallas_call x1, Pallas kernels: 97.2 us -> 68.4 us  [local(): pl.pallas_call(functools.partial(kernel, n, nv), out_shape=jax.ShapeDtype...]
where the time goes in v1:
time: 71.8 us; the launch traced here: 71.6 us
  Pallas kernels  68.4 us (95%)
  local copies, waits for them, and re-layouts  2.49 us (3%)
    pallas_call x1, Pallas kernels, local(): pl.pallas_call(functools.partial(kernel, n, nv), out_shape=jax.ShapeDtype...  68.4 us

profile of v1, /device:TPU:0, one launch (start us, length us, event | category | flops | bytes accessed | tf_op | source)
XLA Modules:
  0.0 71.6 jit_solution(18402104080419830444)
XLA Ops:
  0.6 68.4 %shard_map.84 = f32[8,128]{1,0:T(8,128)} custom-call(bf16[64,2880]{1,0:T(8,128)(2,1)} %hidden_ref.1, f32[2880]{0:T(1024)} %gain_ref.1, bf16[720,6272]{1,0:T(8,128)(2,1)} %unembed_ref.1, s32[1,256]{1,0:T(1,128)} %bitcast.10, s32[1,256]{1,0:T(1,128)} %bitcast.11), custom_call_target="tpu_custom_call" | custom-call | tf_op jit(solution)/shard_map/pallas_call | solution.py:412
  69.1 1.3 %slice_bitcast_fusion.1 = (f32[64]{0:T(128)}, f32[64]{0:T(128)}, f32[64]{0:T(128)}) fusion(f32[8,128]{1,0:T(8,128)} %shard_map.84), kind=kLoop, calls=%fused_computation.1 | loop fusion | bytes 1536 | tf_op jit(solution)/shard_map/squeeze | solution.py:449
  70.4 1.2 %slice_bitcast_fusion = f32[48]{0:T(128)} fusion(f32[8,128]{1,0:T(8,128)} %shard_map.84), kind=kLoop, calls=%fused_computation | loop fusion | bytes 384 | tf_op jit(solution)/shard_map/squeeze | solution.py:449

commit v2 on v1

v2 whole, which is shorter than its diff:
```python
import functools

import jax
import jax.numpy as jnp
from jax import lax
from jax.experimental import pallas as pl
from jax.experimental.pallas import tpu as pltpu
from jax.sharding import PartitionSpec as P

SEQS = 48
LANES = 128
LAG = 9
GROUPS = 2
PAIR_FROM = 2
PART_ROWS = 8
LOWEST = -1e38
LEVELS = 32760.0
TINY = 1e-30
MESH = pl.DeviceIdType.MESH


def kernel(
    n, nv, hidden_ref, gain_ref, unembed_ref, targets_ref, seq_ref, out_ref,
    weights, blocks, rows_in, buf, part, peaks, bound, steps, target_cols, state, packed, gathered,
    w_sem, own_sem, x_send, x_recv, p_send, p_recv, c_send, c_recv, b_send, b_recv,
    v_send, v_recv,
):
    me = lax.axis_index("width")
    my_vocab = lax.axis_index("vocab")
    own_rows, width_dim = hidden_ref.shape
    share = width_dim // n
    half = (n // 2) * own_rows
    chunks = unembed_ref.shape[1] // LANES
    last = n - 1
    group_blocks = n // 2 // GROUPS
    group_rows = group_blocks * own_rows
    items = GROUPS * chunks
    slots = last * LAG + 1
    tile = tile_of(chunks)
    tiles = chunks // tile

    early = tile * LANES
    loads = []
    for k, cols in enumerate((pl.ds(0, early), pl.ds(early, chunks * LANES - early))):
        loads.append(
            pltpu.make_async_copy(unembed_ref.at[:, cols], weights.at[:, cols], w_sem.at[k])
        )
        loads[k].start()

    barrier = pltpu.get_barrier_semaphore()
    for k in range(1, n):
        pl.semaphore_signal(
            barrier, inc=1, device_id={"width": lax.rem(me + k, n)}, device_id_type=MESH
        )
    for k in range(1, nv):
        pl.semaphore_signal(
            barrier, inc=1, device_id={"vocab": lax.rem(my_vocab + k, nv)}, device_id_type=MESH
        )

    values = hidden_ref[...].astype(jnp.float32)
    square = jnp.mean(values * values, axis=1, keepdims=True)
    normed = (values * lax.rsqrt(square + 1e-05) * gain_ref[...][None, :]).astype(jnp.bfloat16)
    for j in range(n):
        blocks[j] = normed[:, j * share : (j + 1) * share]

    pl.semaphore_wait(barrier, n - 1 + nv - 1)

    parts = parts_of(nv, own_rows)
    part_rows = own_rows // parts
    place = lax.rem(my_vocab, parts)

    def part_of(k):
        return pl.ds(pl.multiple_of(k * part_rows, part_rows), part_rows)

    def row_copy(peer, source):
        return pltpu.make_async_remote_copy(
            src_ref=blocks.at[peer, part_of(place)],
            dst_ref=rows_in.at[source, part_of(place)],
            send_sem=x_send.at[peer],
            recv_sem=x_recv.at[source],
            device_id={"width": peer},
            device_id_type=MESH,
        )

    def pass_rows(source, peer, owner):
        return pltpu.make_async_remote_copy(
            src_ref=rows_in.at[source, part_of(owner)],
            dst_ref=rows_in.at[source, part_of(owner)],
            send_sem=p_send.at[source * parts + peer],
            recv_sem=p_recv.at[source * parts + owner],
            device_id={"vocab": my_vocab - place + peer},
            device_id_type=MESH,
        )

    half_rows = own_rows // 2
    parity = lax.rem(place, 2)
    partner = place + 1 - 2 * parity

    def half_of(k):
        return pl.ds(pl.multiple_of(k * half_rows, half_rows), half_rows)

    def near_copy(peer, source):
        return pltpu.make_async_remote_copy(
            src_ref=blocks.at[peer, half_of(parity)],
            dst_ref=rows_in.at[source, half_of(parity)],
            send_sem=x_send.at[peer],
            recv_sem=x_recv.at[source],
            device_id={"width": peer},
            device_id_type=MESH,
        )

    def near_pass(source, half_index, owner):
        return pltpu.make_async_remote_copy(
            src_ref=rows_in.at[source, half_of(half_index)],
            dst_ref=rows_in.at[source, half_of(half_index)],
            send_sem=p_send.at[source * parts + partner],
            recv_sem=p_recv.at[source * parts + owner],
            device_id={"vocab": my_vocab - place + partner},
            device_id_type=MESH,
        )

    at_end = (me == 0) | (me == last)

    def peer_of(k):
        return lax.rem(me + jnp.where(me < n // 2, k, n - k), n)

    def is_near(source):
        return ((source == 0) & (me == 1)) | ((source == last) & (me == last - 1))

    @pl.when(at_end)
    def _():
        near_copy(peer_of(1), me).start()

    @pl.when(jnp.logical_not(at_end))
    def _():
        row_copy(peer_of(1), me).start()

    for k in range(2, n):
        row_copy(peer_of(k), me).start()

    own = pltpu.make_async_copy(blocks.at[me], rows_in.at[me], own_sem)
    own.start()

    target_row = targets_ref[...].astype(jnp.float32)
    target_all = jnp.transpose(jnp.broadcast_to(target_row, (LANES, 2 * half)))
    target_cols[0] = target_all[:half]
    target_cols[1] = target_all[half:]
    state[0] = jnp.full((half, LANES), LOWEST, jnp.float32)
    for k in range(1, 4):
        state[k] = jnp.zeros((half, LANES), jnp.float32)

    own.wait()
    loads[0].wait()

    def chunk_copy(side, c, peer):
        return pltpu.make_async_remote_copy(
            src_ref=buf.at[side, c],
            dst_ref=buf.at[side, c],
            send_sem=c_send.at[side, lax.rem(c, slots)],
            recv_sem=c_recv.at[side, lax.rem(c, slots)],
            device_id={"width": peer},
            device_id_type=MESH,
        )

    first_col = my_vocab * (chunks * LANES)
    lane = lax.broadcasted_iota(jnp.int32, (half, LANES), 1)
    item_lane = lax.broadcasted_iota(jnp.int32, (group_rows, LANES), 1)

    def bound_copy(side, t, peer):
        return pltpu.make_async_remote_copy(
            src_ref=bound.at[side, t],
            dst_ref=bound.at[side, t],
            send_sem=b_send.at[side, t],
            recv_sem=b_recv.at[side, t],
            device_id={"width": peer},
            device_id_type=MESH,
        )

    def by_vreg(values):
        return values.reshape(group_rows // 8, 8, LANES)

    def keep(side, group, c, t, logits):
        peak = jnp.full((8, LANES), TINY, jnp.float32)
        for j in range(tile):
            piece = logits[:, j * LANES : (j + 1) * LANES]
            part[side, group * chunks + c + j] = piece
            peak = jnp.maximum(peak, jnp.max(jnp.abs(by_vreg(piece)), axis=0))
        peaks[side, t] = peak

    def tile_logits(x, c):
        cols = pl.ds(pl.multiple_of(c * LANES, LANES), tile * LANES)
        x = x.reshape(x.shape[0] * own_rows, share)
        return jnp.dot(x, weights[:, cols], preferred_element_type=jnp.float32)

    def open_tile(side, group, first_block, c, t, head, tail, peer):
        for g in range(GROUPS):
            start = g * group_blocks if side == 0 else n - (g + 1) * group_blocks

            @pl.when(t == g)
            def _():
                for w in range(start, start + group_blocks):
                    if w in (0, last):

                        @pl.when(is_near(w))
                        def _():
                            near_copy(w, w).wait_recv()
                            near_pass(w, parity, place).start()

                    @pl.when((me != w) & jnp.logical_not(is_near(w)))
                    def _():
                        row_copy(w, w).wait_recv()
                        for k in range(1, parts):
                            pass_rows(w, lax.rem(place + k, parts), place).start()

            @pl.when(t == g * PAIR_FROM)
            def _():
                for w in range(start, start + group_blocks):
                    if w in (0, last):

                        @pl.when(is_near(w))
                        def _():
                            near_pass(w, 1 - parity, partner).wait_recv()

                    @pl.when((me != w) & jnp.logical_not(is_near(w)))
                    def _():
                        for k in range(1, parts):
                            other = lax.rem(place + k, parts)
                            pass_rows(w, other, other).wait_recv()

        @pl.when(t - group * tiles < PAIR_FROM)
        def _():
            keep(side, group, c, t, tile_logits(rows_in[pl.ds(first_block, group_blocks)], c))

        @pl.when((group == 0) & (t >= PAIR_FROM))
        def _():
            logits = tile_logits(rows_in[side * (n // 2) : (side + 1) * (n // 2)], c)
            for g in range(GROUPS):
                start = (g if side == 0 else GROUPS - 1 - g) * group_rows
                keep(side, g, c, t + g * tiles, logits[start : start + group_rows])

        def announce(limit):
            bound[side, t] = limit
            steps[side, 1] = LEVELS / limit
            bound_copy(side, t, peer).start()

        @pl.when(me == head)
        def _():
            announce(peaks[side, t])

        @pl.when(me != head)
        def _():
            bound_copy(side, t, peer).wait_recv()
            incoming = bound[side, t]
            steps[side, 0] = incoming * (1.0 / LEVELS)

            @pl.when(me != tail)
            def _():
                announce(incoming + peaks[side, t])

    def to_codes(side, values):
        scaled = by_vreg(values) * steps[side, 1][None]
        return jnp.round(scaled).astype(jnp.int32).astype(jnp.int16).reshape(group_rows, LANES)

    def from_codes(side, codes):
        values = by_vreg(codes.astype(jnp.int32).astype(jnp.float32)) * steps[side, 0][None]
        return values.reshape(group_rows, LANES)

    def take_stats(side, first_block, c, logits):
        rows = pl.ds(pl.multiple_of((first_block - side * (n // 2)) * own_rows, 8), group_rows)
        column = (first_col + c * LANES + item_lane).astype(jnp.float32)
        old_max = state[0, rows]
        new_max = jnp.maximum(old_max, logits)
        scale = jnp.exp(old_max - new_max)
        shifted = jnp.exp(logits - new_max)
        state[0, rows] = new_max
        state[1, rows] = state[1, rows] * scale + shifted
        state[2, rows] = state[2, rows] * scale + shifted * logits
        state[3, rows] = state[3, rows] + jnp.where(column == target_cols[side, rows], logits, 0.0)

    def advance(side, item, head, tail, peer):
        @pl.when((item >= 0) & (item < items))
        def _():
            group = item // chunks
            c = item - group * chunks
            first_block = group * group_blocks if side == 0 else n - (group + 1) * group_blocks
            @pl.when(lax.rem(item, tile) == 0)
            def _():
                open_tile(side, group, first_block, c, item // tile, head, tail, peer)

            @pl.when((me != tail) & (item >= slots))
            def _():
                chunk_copy(side, item - slots, peer).wait_send()

            @pl.when(me == head)
            def _():
                buf[side, item] = to_codes(side, part[side, item])
                chunk_copy(side, item, peer).start()

            @pl.when(me != head)
            def _():
                chunk_copy(side, item, peer).wait_recv()
                total = from_codes(side, buf[side, item]) + part[side, item]

                @pl.when(me != tail)
                def _():
                    buf[side, item] = to_codes(side, total)
                    chunk_copy(side, item, peer).start()

                @pl.when(me == tail)
                def _():
                    take_stats(side, first_block, c, total)

    down = lax.rem(me + n - 1, n)
    up = lax.rem(me + 1, n)

    def step(s, carry):
        @pl.when(s == 1)
        def _():
            loads[1].wait()

        advance(0, s - me * LAG, 0, last, up)
        advance(1, s - (last - me) * LAG, last, 0, down)
        return carry

    lax.fori_loop(0, items + last * LAG, step, 0)

    def stats_copy(side, w, v, source):
        return pltpu.make_async_remote_copy(
            src_ref=packed,
            dst_ref=gathered.at[side, source],
            send_sem=v_send.at[w * nv + v],
            recv_sem=v_recv.at[side * nv + source],
            device_id={"width": w, "vocab": v},
            device_id_type=MESH,
        )

    def for_others(side, act):
        def body(i, carry):
            far = i // nv
            w = far if side == 0 else last - far
            v = lax.rem(my_vocab + lax.rem(i, nv), nv)
            act(stats_copy(side, w, v, my_vocab))
            return carry

        lax.fori_loop(0, last * nv, body, 0)
        for k in range(1, nv):
            act(stats_copy(side, last if side == 0 else 0, lax.rem(my_vocab + k, nv), my_vocab))

    def finish(side):
        lane_max = state[0]
        row_max = jnp.max(lane_max, axis=1, keepdims=True)
        scale = jnp.exp(lane_max - row_max)
        columns = (
            row_max,
            jnp.sum(state[1] * scale, axis=1, keepdims=True),
            jnp.sum(state[2] * scale, axis=1, keepdims=True),
            jnp.sum(state[3], axis=1, keepdims=True),
        )
        wide = jnp.zeros((half, LANES), jnp.float32)
        for k in range(4):
            wide = jnp.where(lane == k, columns[k], wide)
        flat = jnp.transpose(wide)[:4]
        packed[...] = flat
        for_others(side, lambda copy: copy.start())
        gathered[side, my_vocab] = flat

    @pl.when(me == last)
    def _():
        finish(0)

    @pl.when(me == 0)
    def _():
        finish(1)

    def results(side):
        @pl.when(me != (last if side == 0 else 0))
        def _():
            stats_copy(side, me, my_vocab, my_vocab).wait_recv()

        for k in range(1, nv):
            stats_copy(side, me, my_vocab, lax.rem(my_vocab + k, nv)).wait_recv()

        pieces = [gathered[side, v] for v in range(nv)]
        top = functools.reduce(jnp.maximum, [piece[0:1] for piece in pieces])
        total = jnp.zeros_like(top)
        weighted = jnp.zeros_like(top)
        target = jnp.zeros_like(top)
        for piece in pieces:
            factor = jnp.exp(piece[0:1] - top)
            total = total + piece[1:2] * factor
            weighted = weighted + piece[2:3] * factor
            target = target + piece[3:4]
        log_normalizer = top + jnp.log(total)
        return log_normalizer, log_normalizer - weighted / total, target - log_normalizer

    final = [results(0), results(1)]

    ids = lax.broadcasted_iota(jnp.int32, (LANES, half), 0)
    sums = jnp.zeros((LANES, 1), jnp.float32)
    counts = jnp.zeros((LANES, 1), jnp.float32)
    for side in range(2):
        in_sequence = ids == seq_ref[:, side * half : (side + 1) * half]
        sums = sums + jnp.sum(jnp.where(in_sequence, final[side][2], 0.0), axis=1, keepdims=True)
        counts = counts + jnp.sum(in_sequence.astype(jnp.float32), axis=1, keepdims=True)
    means = sums / jnp.maximum(counts, 1.0)
    out_ref[...] = jnp.zeros_like(out_ref)
    out_ref[3:4, :] = jnp.transpose(jnp.broadcast_to(means, (LANES, LANES)))[0:1]
    for w in range(n):

        @pl.when(me == w)
        def _():
            start = (w % (n // 2)) * own_rows
            for k in range(3):
                mine = final[w // (n // 2)][k][:, start : start + own_rows]
                out_ref[k : k + 1, 0:own_rows] = mine

    @pl.when(at_end)
    def _():
        near_copy(peer_of(1), me).wait_send()

    @pl.when(jnp.logical_not(at_end))
    def _():
        row_copy(peer_of(1), me).wait_send()

    for k in range(2, n):
        row_copy(peer_of(k), me).wait_send()

    for k in range(1, n):
        source = lax.rem(me + k, n)

        @pl.when(is_near(source))
        def _():
            near_pass(source, parity, place).wait_send()

        @pl.when(jnp.logical_not(is_near(source)))
        def _():
            for j in range(1, parts):
                pass_rows(source, lax.rem(place + j, parts), place).wait_send()

    def drain(c, carry):
        @pl.when(me != last)
        def _():
            chunk_copy(0, c, up).wait_send()

        @pl.when(me != 0)
        def _():
            chunk_copy(1, c, down).wait_send()

        return carry

    lax.fori_loop(max(items - slots, 0), items, drain, 0)

    def drain_bounds(t, carry):
        @pl.when(me != last)
        def _():
            bound_copy(0, t, up).wait_send()

        @pl.when(me != 0)
        def _():
            bound_copy(1, t, down).wait_send()

        return carry

    lax.fori_loop(0, items // tile, drain_bounds, 0)

    @pl.when(me == last)
    def _():
        for_others(0, lambda copy: copy.wait_send())

    @pl.when(me == 0)
    def _():
        for_others(1, lambda copy: copy.wait_send())


def split_outputs(packed_ref, *refs):
    for k, ref in enumerate(refs):
        ref[...] = packed_ref[k : k + 1, : ref.shape[1]]


def tile_of(chunks):
    return max(k for k in range(1, 9) if chunks % k == 0)


def parts_of(nv, own_rows):
    return min(nv, own_rows // PART_ROWS)


def solution(mesh):
    n, nv = mesh.shape["width"], mesh.shape["vocab"]

    def local(hidden, gain, unembed, targets, seq_ids):
        own_rows, width_dim = hidden.shape
        share, columns = unembed.shape
        half = (n // 2) * own_rows
        items = GROUPS * (columns // LANES)
        tile = tile_of(columns // LANES)
        vmem = pl.BlockSpec(memory_space=pltpu.VMEM)
        out = pl.pallas_call(
            functools.partial(kernel, n, nv),
            out_shape=jax.ShapeDtypeStruct((8, LANES), jnp.float32),
            in_specs=[vmem, vmem, pl.BlockSpec(memory_space=pl.ANY), vmem, vmem],
            out_specs=vmem,
            scratch_shapes=[
                pltpu.VMEM((share, columns), jnp.bfloat16),
                pltpu.VMEM((n, own_rows, share), jnp.bfloat16),
                pltpu.VMEM((n, own_rows, share), jnp.bfloat16),
                pltpu.VMEM((2, items, half // GROUPS, LANES), jnp.int16),
                pltpu.VMEM((2, items, half // GROUPS, LANES), jnp.float32),
                pltpu.VMEM((2, items // tile, 8, LANES), jnp.float32),
                pltpu.VMEM((2, items // tile, 8, LANES), jnp.float32),
                pltpu.VMEM((2, 2, 8, LANES), jnp.float32),
                pltpu.VMEM((2, half, LANES), jnp.float32),
                pltpu.VMEM((4, half, LANES), jnp.float32),
                pltpu.VMEM((4, half), jnp.float32),
                pltpu.VMEM((2, nv, 4, half), jnp.float32),
                pltpu.SemaphoreType.DMA((2,)),
                pltpu.SemaphoreType.DMA,
                pltpu.SemaphoreType.DMA((n,)),
                pltpu.SemaphoreType.DMA((n,)),
                pltpu.SemaphoreType.DMA((n * parts_of(nv, own_rows),)),
                pltpu.SemaphoreType.DMA((n * parts_of(nv, own_rows),)),
                pltpu.SemaphoreType.DMA((2, (n - 1) * LAG + 1)),
                pltpu.SemaphoreType.DMA((2, (n - 1) * LAG + 1)),
                pltpu.SemaphoreType.DMA((2, items // tile)),
                pltpu.SemaphoreType.DMA((2, items // tile)),
                pltpu.SemaphoreType.DMA((n * nv,)),
                pltpu.SemaphoreType.DMA((2 * nv,)),
            ],
            compiler_params=pltpu.CompilerParams(
                collective_id=0, has_side_effects=True, vmem_limit_bytes=66_000_000
            ),
        )(hidden, gain, unembed, targets[None, :], seq_ids[None, :])
        split = pl.pallas_call(
            split_outputs,
            out_shape=[jax.ShapeDtypeStruct((1, k), jnp.float32) for k in 3 * [own_rows] + [SEQS]],
            in_specs=[vmem],
            out_specs=[vmem] * 4,
        )(out)
        return tuple(array[0] for array in split)

    return jax.shard_map(
        local,
        mesh=mesh,
        in_specs=(P("width", None), P(), P("width", "vocab"), P(), P()),
        out_specs=(P("width"), P("width"), P("width"), P()),
        check_vma=False,
    )
```

time: 71.8 us -> 67.2 us (0.936)
  local copies, waits for them, and re-layouts: 2.49 us -> 0 us
  Pallas kernels: 68.4 us -> 66.4 us
    pallas_call x1, Pallas kernels: 68.4 us -> 65.2 us  [local(): pl.pallas_call(functools.partial(kernel, n, nv), out_shape=jax.ShapeDtype...]
    squeeze x2 -> x0, local copies, waits for them, and re-layouts: 2.49 us -> none  [the longest x1 1.3 us: local(): out[2, :own_rows]]
    pallas_call x0 -> x1, Pallas kernels: none -> 1.2 us  [local(): pl.pallas_call(split_outputs, out_shape=[jax.ShapeDtypeStruct((1, k), jnp...]
where the time goes in v2:
time: 67.2 us; the launch traced here: 67 us
  Pallas kernels  66.4 us (99%)
    pallas_call x1, Pallas kernels, local(): pl.pallas_call(functools.partial(kernel, n, nv), out_shape=jax.ShapeDtype...  65.2 us

profile of v2, /device:TPU:0, one launch (start us, length us, event | category | flops | bytes accessed | tf_op | source)
XLA Modules:
  0.0 67.0 jit_solution(1832732053722980753)
XLA Ops:
  0.6 65.2 %shard_map.84.packed_ref = f32[8,128]{1,0:T(8,128)} custom-call(bf16[64,2880]{1,0:T(8,128)(2,1)} %hidden_ref.1, f32[2880]{0:T(1024)} %gain_ref.1, bf16[720,6272]{1,0:T(8,128)(2,1)} %unembed_ref.1, s32[1,256]{1,0:T(1,128)} %bitcast.6, s32[1,256]{1,0:T(1,128)} %bitcast.7), custom_call_target="tpu_custom_call" | custom-call | tf_op jit(solution)/shard_map/pallas_call | solution.py:498
  65.8 1.2 %shard_map.85 = (f32[1,64]{1,0:T(1,128)}, f32[1,64]{1,0:T(1,128)}, f32[1,64]{1,0:T(1,128)}, f32[1,48]{1,0:T(1,128)}) custom-call(f32[8,128]{1,0:T(8,128)} %shard_map.84.packed_ref), custom_call_target="tpu_custom_call" | custom-call | tf_op jit(solution)/shard_map/pallas_call | solution.py:533

commit v3 on v2

--- a/solution.py
+++ b/solution.py
@@ -196,22 +196,6 @@
         for g in range(GROUPS):
             start = g * group_blocks if side == 0 else n - (g + 1) * group_blocks
 
-            @pl.when(t == g)
-            def _():
-                for w in range(start, start + group_blocks):
-                    if w in (0, last):
-
-                        @pl.when(is_near(w))
-                        def _():
-                            near_copy(w, w).wait_recv()
-                            near_pass(w, parity, place).start()
-
-                    @pl.when((me != w) & jnp.logical_not(is_near(w)))
-                    def _():
-                        row_copy(w, w).wait_recv()
-                        for k in range(1, parts):
-                            pass_rows(w, lax.rem(place + k, parts), place).start()
-
             @pl.when(t == g * PAIR_FROM)
             def _():
                 for w in range(start, start + group_blocks):
@@ -313,7 +297,36 @@
     down = lax.rem(me + n - 1, n)
     up = lax.rem(me + 1, n)
 
+    def take_near(w):
+        @pl.when(is_near(w))
+        def _():
+            near_copy(w, w).wait_recv()
+            near_pass(w, parity, place).start()
+
+    def take_rows(sources, here):
+        for w in sources:
+
+            @pl.when(here & (me != w) & jnp.logical_not(is_near(w)))
+            def _():
+                row_copy(w, w).wait_recv()
+                for k in range(1, parts):
+                    pass_rows(w, lax.rem(place + k, parts), place).start()
+
+    take_near(0)
+    take_near(last)
+    take_rows([*range(1, last), 0, last], jnp.logical_not(at_end))
+
     def step(s, carry):
+        @pl.when((s == tile) & at_end)
+        def _():
+            take_rows(range(1, n // 2), me == 0)
+            take_rows(range(n // 2, last), me == last)
+
+        @pl.when((s == 2 * tile) & at_end)
+        def _():
+            take_rows(range(n // 2, n), me == 0)
+            take_rows(range(n // 2), me == last)
+
         @pl.when(s == 1)
         def _():
             loads[1].wait()

time: 67.2 us -> 63.7 us (0.948)
  Pallas kernels: 66.4 us -> 62.9 us
    pallas_call x1, Pallas kernels: 65.2 us -> 61.7 us  [local(): pl.pallas_call(functools.partial(kernel, n, nv), out_shape=jax.ShapeDtype...]
where the time goes in v3:
time: 63.7 us; the launch traced here: 63.5 us
  Pallas kernels  62.9 us (99%)
  between operations  0.64 us (1%)
    pallas_call x1, Pallas kernels, local(): pl.pallas_call(functools.partial(kernel, n, nv), out_shape=jax.ShapeDtype...  61.7 us

profile of v3, /device:TPU:0, one launch (start us, length us, event | category | flops | bytes accessed | tf_op | source)
XLA Modules:
  0.0 63.5 jit_solution(9039980640159197143)
XLA Ops:
  0.6 61.7 %shard_map.84.packed_ref = f32[8,128]{1,0:T(8,128)} custom-call(bf16[64,2880]{1,0:T(8,128)(2,1)} %hidden_ref.1, f32[2880]{0:T(1024)} %gain_ref.1, bf16[720,6272]{1,0:T(8,128)(2,1)} %unembed_ref.1, s32[1,256]{1,0:T(1,128)} %bitcast.6, s32[1,256]{1,0:T(1,128)} %bitcast.7), custom_call_target="tpu_custom_call" | custom-call | tf_op jit(solution)/shard_map/pallas_call | solution.py:511
  62.3 1.2 %shard_map.85 = (f32[1,64]{1,0:T(1,128)}, f32[1,64]{1,0:T(1,128)}, f32[1,64]{1,0:T(1,128)}, f32[1,48]{1,0:T(1,128)}) custom-call(f32[8,128]{1,0:T(8,128)} %shard_map.84.packed_ref), custom_call_target="tpu_custom_call" | custom-call | tf_op jit(solution)/shard_map/pallas_call | solution.py:546
